TPU v7x, 512 devices: a whole 4x8x8 slice. The times are simulated.
512 devices in a mesh: lat: 32 (over z, y_hi, core), lon: 16 (over y_lo, x).
Axes of the slice: x: 4, y: 8 (y_hi: 2, y_lo: 4; y = y_hi * 4 + y_lo), z: 8, core: 2. Of those that a mesh axis runs over, the one named last changes fastest.
Arguments:
- fields: float32 [5, 32, 32, 4096], P(None, None, 'lat', 'lon'), may hold values from -6 to 6
- east_courant: float32 [32, 32, 4096], P(None, 'lat', 'lon'), may hold values from -0.45 to 0.45
- north_courant: float32 [32, 32, 4096], P(None, 'lat', 'lon'), may hold values from -0.45 to 0.45
- offsets: int32 [32], P('lat'), may hold values from -8 to 7
- lower_blocks: float32 [5, 5, 31, 32], P(None, None, None, 'lat'), may hold values from -0.4 to 0.4
- pivot_inverse: float32 [5, 5, 32, 32], P(None, None, None, 'lat'), may hold values from -0.36 to 1, as said below
- upper_blocks: float32 [5, 5, 31, 32], P(None, None, None, 'lat'), may hold values from -0.4 to 0.4
Outputs:
- solved: float32 [5, 32, 32, 4096], P(None, None, 'lat', 'lon')
Inputs may be any that keep to these rules, and one draw needn't show every extreme that they name: `pivot_inverse`: diagonal entries of each 5 x 5 block lie between 0.3 and 1; off-diagonal entries are at most 0.36 in magnitude.
All inputs are finite; a program needn't handle non-finite values.
Results may differ from a plain program's by a relative error of at most 0.0001.
Values sent between devices are 32-bit elements; how exact they have to be, the bound alone decides.
A program may use at most 64 MiB of HBM per device.

v0:
```python
import jax
import jax.numpy as jnp
from jax import lax
from jax.sharding import PartitionSpec as P


def padded(block, sides, width, periodic):
    for axis, dim in sides:
        count = lax.axis_size(axis)
        forward = [(i, i + 1) for i in range(count - 1)]
        if periodic:
            forward.append((count - 1, 0))
        backward = [(target, source) for source, target in forward]
        low = lax.ppermute(
            lax.slice_in_dim(block, block.shape[dim] - width, None, axis=dim), axis, forward
        )
        high = lax.ppermute(lax.slice_in_dim(block, 0, width, axis=dim), axis, backward)
        block = jnp.concatenate([low, block, high], axis=dim)
    return block


def apply_block(block, vector):
    return jnp.einsum("abj,bji->aji", block, vector, precision=lax.Precision.HIGHEST)


def column_solve(advected, lower_blocks, pivot_inverse, upper_blocks):
    first = apply_block(pivot_inverse[:, :, 0], advected[:, 0])

    def forward_step(previous, inputs):
        right, lower, pivot = inputs
        current = apply_block(pivot, right - apply_block(lower, previous))
        return (current, current)

    inputs = (
        jnp.moveaxis(advected[:, 1:], 1, 0),
        jnp.moveaxis(lower_blocks, 2, 0),
        jnp.moveaxis(pivot_inverse[:, :, 1:], 2, 0),
    )
    last, rest = lax.scan(forward_step, first, inputs)
    forward = jnp.concatenate([first[None], rest], axis=0)

    def backward_step(following, inputs):
        current_forward, upper = inputs
        current = current_forward - apply_block(upper, following)
        return (current, current)

    top, lower_rest = lax.scan(
        backward_step, last, (forward[:-1], jnp.moveaxis(upper_blocks, 2, 0)), reverse=True
    )
    solved = jnp.concatenate([lower_rest, last[None]], axis=0)
    return jnp.moveaxis(solved, 0, 1)


def body(fields, east_courant, north_courant, offsets, lower_blocks, pivot_inverse, upper_blocks):
    cycle_count = lax.axis_size("lon")
    cycle_place = lax.axis_index("lon")
    band_place = lax.axis_index("lat")
    row_count = fields.shape[2]
    width = fields.shape[3]
    field_count = fields.shape[0]
    displace = jnp.mod(offsets, cycle_count)
    wanted = jnp.mod(cycle_place - displace, cycle_count)
    piece = lax.all_gather(fields, "lon", axis=3, tiled=True)
    span = piece.shape[3]
    begin = wanted * width
    valid = (begin >= 0) & (begin <= span - width)
    safe = jnp.clip(begin, 0, span - width)

    def one_row(block, anchor):
        return lax.dynamic_slice_in_dim(block, anchor, width, 2)

    taken = jax.vmap(one_row, in_axes=(2, 0), out_axes=2)(piece, safe)
    moved = jnp.where(valid[None, None, :, None], taken, 0.0)
    global_rows = band_place * row_count + jnp.arange(row_count, dtype=jnp.int32)
    total_rows = row_count * lax.axis_size("lat")
    north_wall = jnp.where((global_rows == total_rows - 1)[None, :, None], 0.0, north_courant)
    lat_stack = jnp.concatenate([moved, north_wall[None]], axis=0)
    lon_stack = jnp.concatenate([moved, east_courant[None]], axis=0)
    lat_padded = padded(lat_stack, (("lat", 2),), 1, False)
    lon_padded = padded(lon_stack, (("lon", 3),), 1, True)
    east_flux = (
        jnp.maximum(east_courant, 0.0) * moved
        + jnp.minimum(east_courant, 0.0) * lon_padded[:field_count, :, :, 2:]
    )
    west_courant = lon_padded[field_count, :, :, :-2]
    west_flux = (
        jnp.maximum(west_courant, 0.0) * lon_padded[:field_count, :, :, :-2]
        + jnp.minimum(west_courant, 0.0) * moved
    )
    north_flux = (
        jnp.maximum(north_wall, 0.0) * moved
        + jnp.minimum(north_wall, 0.0) * lat_padded[:field_count, :, 2:, :]
    )
    south_courant = lat_padded[field_count, :, :-2, :]
    south_flux = (
        jnp.maximum(south_courant, 0.0) * lat_padded[:field_count, :, :-2, :]
        + jnp.minimum(south_courant, 0.0) * moved
    )
    advected = moved - (east_flux - west_flux) - (north_flux - south_flux)
    return column_solve(advected, lower_blocks, pivot_inverse, upper_blocks)


def solution(mesh):
    in_specs = (
        P(None, None, "lat", "lon"),
        P(None, "lat", "lon"),
        P(None, "lat", "lon"),
        P("lat"),
        P(None, None, None, "lat"),
        P(None, None, None, "lat"),
        P(None, None, None, "lat"),
    )
    out_specs = P(None, None, "lat", "lon")
    return jax.shard_map(body, mesh=mesh, in_specs=in_specs, out_specs=out_specs, check_vma=False)
```

profile of v0, /device:TPU:62, one launch (start us, length us, event | category | flops | bytes accessed | tf_op | source)
XLA Modules:
  0.0 152.5 jit_solution(4412390770514833927)
XLA Ops:
  6.5 1.7 %copy.14 = f32[5,32,1,256]{3,0,2,1:T(8,128)} copy(f32[5,32,1,256]{3,2,1,0:T(1,128)} %param.11) | data formatting | bytes 327680 | tf_op args[0]
  9.0 0.8 slice.53
  9.8 0.8 copy.31
  10.7 0.1 copy.17
  10.8 0.9 copy.16
  11.7 0.9 copy.18
  12.5 0.8 broadcast_maximum_fusion.2
  13.3 0.8 broadcast_maximum_fusion.1
  14.2 88.7 %all-gather.2.cloned.1.call-done = f32[5,32,1,4096]{3,0,2,1:T(8,128)} async-done(((f32[5,32,1,256]{3,0,2,1:T(8,128)}), f32[5,32,1,4096]{3,0,2,1:T(8,128)}) %all-gather.2.cloned.1.call-update) | async-done | bytes 2621456 | tf_op jit(solution)/shard_map/all_gather | solution.py:63
  102.9 1.1 dynamic-slice_select_fusion
  104.1 0.9 fusion.25
  104.9 4.4 %collective-permute-start.1 = (f32[6,32,1,1]{3,0,2,1:T(8,128)S(1)}, f32[6,32,1,1]{3,0,2,1:T(8,128)S(1)}, u32[]{:S(2)}, u32[]{:S(2)}) collective-permute-start(f32[6,32,1,1]{3,0,2,1:T(8,128)S(1)} %get-tuple-element.182), channel_id=1, source_target_pairs={{0,1},{1,2},{2,3},{3,4},{4,5},{5,6},{6,7},{7,8},{8,9},{9,10},{10,1... | collective-permute-start | bytes 2312 | tf_op jit(solution)/shard_map/ppermute | solution.py:14
  109.4 1.9 %collective-permute-start.3 = (f32[6,32,1,256]{3,0,2,1:T(8,128)S(1)}, f32[6,32,1,256]{3,0,2,1:T(8,128)S(1)}, u32[]{:S(2)}, u32[]{:S(2)}) collective-permute-start(f32[6,32,1,256]{3,0,2,1:T(8,128)S(1)} %pad_maximum_fusion.4), channel_id=1, source_target_pairs={{0,16},{16,32},{32,48},{48,64},{64,80},{80,96},{96,112},{112,128},... | collective-permute-start | bytes 589832 | tf_op jit(solution)/shard_map/ppermute | solution.py:14
  111.3 7.5 %collective-permute-start.2 = (f32[6,32,1,256]{3,0,2,1:T(8,128)S(1)}, f32[6,32,1,256]{3,0,2,1:T(8,128)S(1)}, u32[]{:S(2)}, u32[]{:S(2)}) collective-permute-start(f32[6,32,1,256]{3,0,2,1:T(8,128)S(1)} %pad_maximum_fusion.4), channel_id=1, source_target_pairs={{16,0},{32,16},{48,32},{64,48},{80,64},{96,80},{112,96},{128,112},... | collective-permute-start | bytes 589832 | tf_op jit(solution)/shard_map/ppermute | solution.py:17
  118.9 1.9 %collective-permute-start = (f32[6,32,1,1]{3,0,2,1:T(8,128)S(1)}, f32[6,32,1,1]{3,0,2,1:T(8,128)S(1)}, u32[]{:S(2)}, u32[]{:S(2)}) collective-permute-start(f32[6,32,1,1]{3,0,2,1:T(8,128)S(1)} %get-tuple-element.181), channel_id=1, source_target_pairs={{1,0},{2,1},{3,2},{4,3},{5,4},{6,5},{7,6},{8,7},{9,8},{10,9},{11,1... | collective-permute-start | bytes 2312 | tf_op jit(solution)/shard_map/ppermute | solution.py:17
  120.8 1.0 broadcast_maximum_fusion
  121.8 0.8 collective-permute-done.3
  122.7 6.9 %collective-permute-done = f32[6,32,1,1]{3,0,2,1:T(8,128)S(1)} collective-permute-done((f32[6,32,1,1]{3,0,2,1:T(8,128)S(1)}, f32[6,32,1,1]{3,0,2,1:T(8,128)S(1)}, u32[]{:S(2)}, u32[]{:S(2)}) %collective-permute-start) | collective-permute-done | bytes 800 | tf_op jit(solution)/shard_map/ppermute | solution.py:17
  129.6 0.4 fusion.17
  130.2 8.8 %while.29 = (s32[]{:T(128)}, f32[5,1,256]{2,0,1:T(8,128)S(1)}, f32[31,5,1,256]{3,1,2,0:T(8,128)S(1)}, f32[31,5,1,256]{3,1,2,0:T(8,128)S(1)}, f32[31,5,5,1]{2,1,3...) while((s32[]{:T(128)}, f32[5,1,256]{2,0,1:T(8,128)S(1)}, f32[31,5,1,256]{3,1,2,0:T(8,128)S(1)}, ...), condition=%wide.region_1.2_spmd, body=%wide.region_0.1_spmd.sunk | while | flops 154882 | bytes 56397 | solution.py:39
  130.5 0.1 fusion.40
  130.8 0.1 fusion.40
  131.1 0.1 fusion.40
  131.3 0.1 fusion.40
  133.0 0.1 fusion.40
  133.3 0.1 fusion.40
  135.9 0.1 fusion.40
  136.2 0.1 fusion.40
  138.4 0.1 fusion.40
  138.7 0.1 fusion.40
  139.1 5.7 %while.30 = (s32[]{:T(128)}, f32[5,1,256]{2,0,1:T(8,128)S(1)}, f32[31,5,1,256]{3,2,0,1:T(1,128)S(1)}, f32[31,5,1,256]{3,1,2,0:T(8,128)S(1)}, f32[31,5,5,1]{2,1,3,0:T(8,128)S(1)}, /*index=5*/s32[]{:T(128)}, s32[]{:T(128)}) while((s32[]{:T(128)}, f32[5,1,256]{2,0,1:T(8,128)S(1)}, f32[31,5,1,256]{3,2,0,1:T(1,128)S(1)}, ...), condition=%wide.region_3.4_spmd, body=%wide.region_2.3_spmd.sunk | while | flops 78083 | bytes 50269 | solution.py:47
  144.8 0.8 maximum_bitcast_fusion
  (165 shorter events, 12.6 us)
Async XLA Ops:
  6.5 123.1 %copy-start = (f32[32,1,256]{2,1,0:T(1,128)S(1)}, f32[32,1,256]{2,1,0:T(1,128)}, u32[]{:S(2)}) copy-start(f32[32,1,256]{2,1,0:T(1,128)} %param.12) | copy-start | bytes 98308
  6.5 96.4 %all-gather.2.cloned.1.call-start = ((), (), s32[]{:S(2)}) async-start(), calls=%async_computation | async-start | bytes 4456448 | tf_op jit(solution)/shard_map/all_gather | solution.py:63
  104.9 15.8 %collective-permute-start.1 = (f32[6,32,1,1]{3,0,2,1:T(8,128)S(1)}, f32[6,32,1,1]{3,0,2,1:T(8,128)S(1)}, u32[]{:S(2)}, u32[]{:S(2)}) collective-permute-start(f32[6,32,1,1]{3,0,2,1:T(8,128)S(1)} %get-tuple-element.182), channel_id=1, source_target_pairs={{0,1},{1,2},{2,3},{3,4},{4,5},{5,6},{6,7},{7,8},{8,9},{9,10},{10,1... | collective-permute-start | bytes 2312 | tf_op jit(solution)/shard_map/ppermute | solution.py:14
  109.4 13.3 %collective-permute-start.3 = (f32[6,32,1,256]{3,0,2,1:T(8,128)S(1)}, f32[6,32,1,256]{3,0,2,1:T(8,128)S(1)}, u32[]{:S(2)}, u32[]{:S(2)}) collective-permute-start(f32[6,32,1,256]{3,0,2,1:T(8,128)S(1)} %pad_maximum_fusion.4), channel_id=1, source_target_pairs={{0,16},{16,32},{32,48},{48,64},{64,80},{80,96},{96,112},{112,128},... | collective-permute-start | bytes 589832 | tf_op jit(solution)/shard_map/ppermute | solution.py:14
  111.3 18.3 %collective-permute-start.2 = (f32[6,32,1,256]{3,0,2,1:T(8,128)S(1)}, f32[6,32,1,256]{3,0,2,1:T(8,128)S(1)}, u32[]{:S(2)}, u32[]{:S(2)}) collective-permute-start(f32[6,32,1,256]{3,0,2,1:T(8,128)S(1)} %pad_maximum_fusion.4), channel_id=1, source_target_pairs={{16,0},{32,16},{48,32},{64,48},{80,64},{96,80},{112,96},{128,112},... | collective-permute-start | bytes 589832 | tf_op jit(solution)/shard_map/ppermute | solution.py:17
  118.9 10.8 %collective-permute-start = (f32[6,32,1,1]{3,0,2,1:T(8,128)S(1)}, f32[6,32,1,1]{3,0,2,1:T(8,128)S(1)}, u32[]{:S(2)}, u32[]{:S(2)}) collective-permute-start(f32[6,32,1,1]{3,0,2,1:T(8,128)S(1)} %get-tuple-element.181), channel_id=1, source_target_pairs={{1,0},{2,1},{3,2},{4,3},{5,4},{6,5},{7,6},{8,7},{9,8},{10,9},{11,1... | collective-permute-start | bytes 2312 | tf_op jit(solution)/shard_map/ppermute | solution.py:17
Sparse Core Ops, SparseCore 0:
  9.4 93.4 all-gather.1
where the time goes:
time: 153 us; the launch traced here: 152 us
  waiting for transfers between devices  96.5 us (63%)
  starting transfers between devices  15.8 us (10%)
  between operations  14.3 us (9%)
  matrix products  13.1 us (9%)
  other arithmetic  6.02 us (4%)
  local copies, waits for them, and re-layouts  5.95 us (4%)
    all_gather x1, waiting for transfers between devices, body(): piece = lax.all_gather(fields, 'lon', axis=3, tiled=True)  88.7 us
    dot_general x94, matrix products, apply_block(): jnp.einsum('abj,bji->aji', block, vector, precision=lax.Precision.HIGHEST)  13.1 us
    ppermute x2, starting transfers between devices, padded(): lax.ppermute(lax.slice_in_dim(block, 0, width, axis=dim), axis, backward)  9.47 us
    ppermute x2, waiting for transfers between devices, padded(): lax.ppermute(lax.slice_in_dim(block, 0, width, axis=dim), axis, backward)  6.91 us
    ppermute x2, starting transfers between devices, padded(): lax.ppermute(lax.slice_in_dim(block, block.shape[dim] - width, None, axis...  6.28 us
    unnamed x11, local copies, waits for them, and re-layouts  4.32 us
  transfers between devices with their start and end apart: 5, of which 3 were waited for; matrix products, arithmetic and copies ran while one was open for 4% of the time, Pallas kernels for 0%

commit v1 on v0

--- a/solution.py
+++ b/solution.py
@@ -53,24 +53,20 @@
 
 def body(fields, east_courant, north_courant, offsets, lower_blocks, pivot_inverse, upper_blocks):
     cycle_count = lax.axis_size("lon")
-    cycle_place = lax.axis_index("lon")
     band_place = lax.axis_index("lat")
     row_count = fields.shape[2]
-    width = fields.shape[3]
     field_count = fields.shape[0]
     displace = jnp.mod(offsets, cycle_count)
-    wanted = jnp.mod(cycle_place - displace, cycle_count)
-    piece = lax.all_gather(fields, "lon", axis=3, tiled=True)
-    span = piece.shape[3]
-    begin = wanted * width
-    valid = (begin >= 0) & (begin <= span - width)
-    safe = jnp.clip(begin, 0, span - width)
 
-    def one_row(block, anchor):
-        return lax.dynamic_slice_in_dim(block, anchor, width, 2)
+    def shift_by(step):
+        pairs = [(place, (place + step) % cycle_count) for place in range(cycle_count)]
 
-    taken = jax.vmap(one_row, in_axes=(2, 0), out_axes=2)(piece, safe)
-    moved = jnp.where(valid[None, None, :, None], taken, 0.0)
+        def branch(block):
+            return block if step == 0 else lax.ppermute(block, "lon", pairs)
+
+        return branch
+
+    moved = lax.switch(displace[0], [shift_by(step) for step in range(cycle_count)], fields)
     global_rows = band_place * row_count + jnp.arange(row_count, dtype=jnp.int32)
     total_rows = row_count * lax.axis_size("lat")
     north_wall = jnp.where((global_rows == total_rows - 1)[None, :, None], 0.0, north_courant)

time: 153 us -> 55.7 us (0.36)
  the two profiles are of different devices: /device:TPU:62 before, /device:TPU:222 now
where the time goes in v1:
time: 55.7 us; the launch traced here: 55.3 us
  starting transfers between devices  21.8 us (39%)
  waiting for transfers between devices  13.3 us (24%)
  matrix products  13.1 us (24%)
  local copies, waits for them, and re-layouts  3.29 us (6%)
  other arithmetic  1.88 us (3%)
  loops' own time  0.97 us (2%)
  between operations  0.92 us (2%)
    dot_general x94, matrix products, apply_block(): jnp.einsum('abj,bji->aji', block, vector, precision=lax.Precision.HIGHEST)  13.1 us
    ppermute x2, starting transfers between devices, padded(): lax.ppermute(lax.slice_in_dim(block, 0, width, axis=dim), axis, backward)  10.4 us
    ppermute x2, starting transfers between devices, padded(): lax.ppermute(lax.slice_in_dim(block, block.shape[dim] - width, None, axis...  8.39 us
    ppermute x1, waiting for transfers between devices, branch(): return block if step == 0 else lax.ppermute(block, 'lon', pairs)  7.35 us
    ppermute x2, waiting for transfers between devices, padded(): lax.ppermute(lax.slice_in_dim(block, 0, width, axis=dim), axis, backward)  5.9 us
    ppermute x1, starting transfers between devices, branch(): return block if step == 0 else lax.ppermute(block, 'lon', pairs)  3.09 us
    unnamed x18, local copies, waits for them, and re-layouts  2.27 us
  transfers between devices with their start and end apart: 5, of which 2 were waited for; matrix products, arithmetic and copies ran while one was open for 2% of the time, Pallas kernels for 0%

profile of v1, /device:TPU:222, one launch (start us, length us, event | category | flops | bytes accessed | tf_op | source)
XLA Modules:
  0.0 55.3 jit_solution(8832076817047888525)
XLA Ops:
  0.7 10.6 %conditional.1 = (f32[5,32,1,256]{3,0,2,1:T(8,128)S(1)}) conditional(s32[]{:T(128)} %bitcast.19, f32[5,32,1,256]{3,2,1,0:T(1,128)} %param.27, f32[5,32,1,256]{3,2,1,0:T(1,128)} %param.27, f32[5,32,1,256]{3,2,1,0:T(1,128)} %param.27, f32[5,32,1,256]{3,2,1,0:T(1,128)} %param.27, f32[5,32,1,256]{3,2,1,0:T(1,128)} %param.27, ...), branch_computations={%region_0.1_spmd, %region_1.2_spmd, %region_2.3_spmd, %region_3.4_... | conditional | bytes 983088 | solution.py:69
  0.7 3.1 %collective-permute-start.5 = (f32[5,32,1,256]{3,2,1,0:T(1,128)}, f32[5,32,1,256]{3,2,1,0:T(1,128)S(1)}, u32[]{:S(2)}, u32[]{:S(2)}) collective-permute-start(f32[5,32,1,256]{3,2,1,0:T(1,128)} %param.6), channel_id=1, source_target_pairs={{0,6},{1,7},{2,8},{3,9},{4,10},{5,11},{6,12},{7,13},{8,14},{9,15},... | collective-permute-start | bytes 491528 | tf_op jit(solution)/shard_map/cond/branch_6_fun/ppermute | solution.py:65
  3.8 7.4 %collective-permute-done.5 = f32[5,32,1,256]{3,2,1,0:T(1,128)S(1)} collective-permute-done((f32[5,32,1,256]{3,2,1,0:T(1,128)}, f32[5,32,1,256]{3,2,1,0:T(1,128)S(1)}, u32[]{:S(2)}, u32[]{:S(2)}) %collective-permute-start.5) | collective-permute-done | bytes 163872 | tf_op jit(solution)/shard_map/cond/branch_6_fun/ppermute | solution.py:65
  11.5 1.9 %collective-permute-start.18 = (f32[6,32,1,256]{3,0,2,1:T(8,128)S(1)}, f32[6,32,1,256]{3,0,2,1:T(8,128)S(1)}, u32[]{:S(2)}, u32[]{:S(2)}) collective-permute-start(f32[6,32,1,256]{3,0,2,1:T(8,128)S(1)} %pad_maximum_fusion.4), channel_id=1, source_target_pairs={{0,16},{16,32},{32,48},{48,64},{64,80},{80,96},{96,112},{112,128},... | collective-permute-start | bytes 589832 | tf_op jit(solution)/shard_map/ppermute | solution.py:14
  13.4 8.4 %collective-permute-start.17 = (f32[6,32,1,256]{3,0,2,1:T(8,128)S(1)}, f32[6,32,1,256]{3,0,2,1:T(8,128)S(1)}, u32[]{:S(2)}, u32[]{:S(2)}) collective-permute-start(f32[6,32,1,256]{3,0,2,1:T(8,128)S(1)} %pad_maximum_fusion.4), channel_id=1, source_target_pairs={{16,0},{32,16},{48,32},{64,48},{80,64},{96,80},{112,96},{128,112},... | collective-permute-start | bytes 589832 | tf_op jit(solution)/shard_map/ppermute | solution.py:17
  22.0 6.5 %collective-permute-start.16 = (f32[6,32,1,1]{3,0,2,1:T(8,128)S(1)}, f32[6,32,1,1]{3,0,2,1:T(8,128)S(1)}, u32[]{:S(2)}, u32[]{:S(2)}) collective-permute-start(f32[6,32,1,1]{3,0,2,1:T(8,128)S(1)} %get-tuple-element.205), channel_id=1, source_target_pairs={{0,1},{1,2},{2,3},{3,4},{4,5},{5,6},{6,7},{7,8},{8,9},{9,10},{10,1... | collective-permute-start | bytes 2312 | tf_op jit(solution)/shard_map/ppermute | solution.py:14
  28.5 1.9 %collective-permute-start.15 = (f32[6,32,1,1]{3,0,2,1:T(8,128)S(1)}, f32[6,32,1,1]{3,0,2,1:T(8,128)S(1)}, u32[]{:S(2)}, u32[]{:S(2)}) collective-permute-start(f32[6,32,1,1]{3,0,2,1:T(8,128)S(1)} %get-tuple-element.204), channel_id=1, source_target_pairs={{1,0},{2,1},{3,2},{4,3},{5,4},{6,5},{7,6},{8,7},{9,8},{10,9},{11,1... | collective-permute-start | bytes 2312 | tf_op jit(solution)/shard_map/ppermute | solution.py:17
  30.5 0.7 %copy-done.1 = f32[5,5,32,1]{2,3,1,0:T(1,128)S(1)} copy-done((f32[5,5,32,1]{2,3,1,0:T(1,128)S(1)}, f32[5,5,32,1]{2,3,1,0:T(1,128)}, u32[]{:S(2)}) %copy-start.1) | copy-done | bytes 3224
  31.4 0.2 copy.29
  31.6 0.6 %copy-done.3 = f32[5,5,31,1]{2,3,1,0:T(1,128)S(1)} copy-done((f32[5,5,31,1]{2,3,1,0:T(1,128)S(1)}, f32[5,5,31,1]{2,3,1,0:T(1,128)}, u32[]{:S(2)}) %copy-start.3) | copy-done | bytes 3124
  32.1 0.1 copy.28
  32.3 0.6 %copy-done.4 = f32[5,5,31,1]{2,3,1,0:T(1,128)S(1)} copy-done((f32[5,5,31,1]{2,3,1,0:T(1,128)S(1)}, f32[5,5,31,1]{2,3,1,0:T(1,128)}, u32[]{:S(2)}) %copy-start.4) | copy-done | bytes 3124
  32.8 0.1 copy.30
  33.0 0.2 broadcast_maximum_fusion
  33.3 5.9 %collective-permute-done.15 = f32[6,32,1,1]{3,0,2,1:T(8,128)S(1)} collective-permute-done((f32[6,32,1,1]{3,0,2,1:T(8,128)S(1)}, f32[6,32,1,1]{3,0,2,1:T(8,128)S(1)}, u32[]{:S(2)}, u32[]{:S(2)}) %collective-permute-start.15) | collective-permute-done | bytes 800 | tf_op jit(solution)/shard_map/ppermute | solution.py:17
  39.2 0.4 fusion.17
  39.8 8.8 %while.28 = (s32[]{:T(128)}, f32[5,1,256]{2,0,1:T(8,128)S(1)}, f32[31,5,1,256]{3,1,2,0:T(8,128)S(1)}, f32[31,5,1,256]{3,1,2,0:T(8,128)S(1)}, f32[31,5,5,1]{2,1,3...) while((s32[]{:T(128)}, f32[5,1,256]{2,0,1:T(8,128)S(1)}, f32[31,5,1,256]{3,1,2,0:T(8,128)S(1)}, ...), condition=%wide.region_17.18_spmd, body=%wide.region_16.17_spmd.sunk | while | flops 154882 | bytes 56397 | solution.py:39
  40.1 0.1 fusion.40
  40.4 0.1 fusion.40
  40.7 0.1 fusion.40
  41.0 0.1 fusion.40
  41.3 0.1 fusion.40
  41.5 0.1 fusion.40
  41.8 0.1 fusion.40
  42.1 0.1 fusion.40
  42.4 0.1 fusion.40
  44.1 0.1 fusion.40
  44.4 0.1 fusion.40
  46.6 0.1 fusion.40
  46.9 0.1 fusion.40
  48.8 5.7 %while.29 = (s32[]{:T(128)}, f32[5,1,256]{2,0,1:T(8,128)S(1)}, f32[31,5,1,256]{3,2,0,1:T(1,128)S(1)}, f32[31,5,1,256]{3,1,2,0:T(8,128)S(1)}, f32[31,5,5,1]{2,1,3,0:T(8,128)S(1)}, /*index=5*/s32[]{:T(128)}, s32[]{:T(128)}) while((s32[]{:T(128)}, f32[5,1,256]{2,0,1:T(8,128)S(1)}, f32[31,5,1,256]{3,2,0,1:T(1,128)S(1)}, ...), condition=%wide.region_19.20_spmd, body=%wide.region_18.19_spmd.sunk | while | flops 78083 | bytes 50269 | solution.py:47
  54.5 0.8 %maximum_bitcast_fusion = f32[5,32,1,256]{3,2,1,0:T(1,128)} fusion(f32[1,5,1,256]{3,2,0,1:T(1,128)S(1)} %reshape_bitcast_fusion, f32[31,5,1,256]{3,2,0,1:T(1,128)S(1)} %get-tuple-element.176), kind=kLoop, calls=%fused_computation.40 | loop fusion | flops 40960 | bytes 327680 | tf_op jit(solution)/shard_map/transpose | solution.py:51
  (172 shorter events, 12.7 us)
Async XLA Ops:
  0.7 10.6 %copy-start.2 = (f32[32,1,256]{2,1,0:T(1,128)S(1)}, f32[32,1,256]{2,1,0:T(1,128)}, u32[]{:S(2)}) copy-start(f32[32,1,256]{2,1,0:T(1,128)} %param.29) | copy-start | bytes 98308
  0.7 10.4 %collective-permute-start.5 = (f32[5,32,1,256]{3,2,1,0:T(1,128)}, f32[5,32,1,256]{3,2,1,0:T(1,128)S(1)}, u32[]{:S(2)}, u32[]{:S(2)}) collective-permute-start(f32[5,32,1,256]{3,2,1,0:T(1,128)} %param.6), channel_id=1, source_target_pairs={{0,6},{1,7},{2,8},{3,9},{4,10},{5,11},{6,12},{7,13},{8,14},{9,15},... | collective-permute-start | bytes 491528 | tf_op jit(solution)/shard_map/cond/branch_6_fun/ppermute | solution.py:65
  11.4 10.5 %copy-start = (f32[32,1,256]{2,1,0:T(1,128)S(1)}, f32[32,1,256]{2,1,0:T(1,128)}, u32[]{:S(2)}) copy-start(f32[32,1,256]{2,1,0:T(1,128)} %param.28) | copy-start | bytes 98308
  11.5 21.8 %collective-permute-start.18 = (f32[6,32,1,256]{3,0,2,1:T(8,128)S(1)}, f32[6,32,1,256]{3,0,2,1:T(8,128)S(1)}, u32[]{:S(2)}, u32[]{:S(2)}) collective-permute-start(f32[6,32,1,256]{3,0,2,1:T(8,128)S(1)} %pad_maximum_fusion.4), channel_id=1, source_target_pairs={{0,16},{16,32},{32,48},{48,64},{64,80},{80,96},{96,112},{112,128},... | collective-permute-start | bytes 589832 | tf_op jit(solution)/shard_map/ppermute | solution.py:14
  13.4 25.9 %collective-permute-start.17 = (f32[6,32,1,256]{3,0,2,1:T(8,128)S(1)}, f32[6,32,1,256]{3,0,2,1:T(8,128)S(1)}, u32[]{:S(2)}, u32[]{:S(2)}) collective-permute-start(f32[6,32,1,256]{3,0,2,1:T(8,128)S(1)} %pad_maximum_fusion.4), channel_id=1, source_target_pairs={{16,0},{32,16},{48,32},{64,48},{80,64},{96,80},{112,96},{128,112},... | collective-permute-start | bytes 589832 | tf_op jit(solution)/shard_map/ppermute | solution.py:17
  22.0 11.0 %collective-permute-start.16 = (f32[6,32,1,1]{3,0,2,1:T(8,128)S(1)}, f32[6,32,1,1]{3,0,2,1:T(8,128)S(1)}, u32[]{:S(2)}, u32[]{:S(2)}) collective-permute-start(f32[6,32,1,1]{3,0,2,1:T(8,128)S(1)} %get-tuple-element.205), channel_id=1, source_target_pairs={{0,1},{1,2},{2,3},{3,4},{4,5},{5,6},{6,7},{7,8},{8,9},{9,10},{10,1... | collective-permute-start | bytes 2312 | tf_op jit(solution)/shard_map/ppermute | solution.py:14
  28.5 10.8 %collective-permute-start.15 = (f32[6,32,1,1]{3,0,2,1:T(8,128)S(1)}, f32[6,32,1,1]{3,0,2,1:T(8,128)S(1)}, u32[]{:S(2)}, u32[]{:S(2)}) collective-permute-start(f32[6,32,1,1]{3,0,2,1:T(8,128)S(1)} %get-tuple-element.204), channel_id=1, source_target_pairs={{1,0},{2,1},{3,2},{4,3},{5,4},{6,5},{7,6},{8,7},{9,8},{10,9},{11,1... | collective-permute-start | bytes 2312 | tf_op jit(solution)/shard_map/ppermute | solution.py:17
  30.5 0.7 %copy-start.1 = (f32[5,5,32,1]{2,3,1,0:T(1,128)S(1)}, f32[5,5,32,1]{2,3,1,0:T(1,128)}, u32[]{:S(2)}) copy-start(f32[5,5,32,1]{2,3,1,0:T(1,128)} %param.32) | copy-start | bytes 9604
  31.4 0.7 %copy-start.3 = (f32[5,5,31,1]{2,3,1,0:T(1,128)S(1)}, f32[5,5,31,1]{2,3,1,0:T(1,128)}, u32[]{:S(2)}) copy-start(f32[5,5,31,1]{2,3,1,0:T(1,128)} %param.31) | copy-start | bytes 9304
  32.1 0.7 %copy-start.4 = (f32[5,5,31,1]{2,3,1,0:T(1,128)S(1)}, f32[5,5,31,1]{2,3,1,0:T(1,128)}, u32[]{:S(2)}) copy-start(f32[5,5,31,1]{2,3,1,0:T(1,128)} %param.33) | copy-start | bytes 9304

commit v2 on v1

v2 whole, which is shorter than its diff:
```python
import jax
import jax.numpy as jnp
from jax import lax
from jax.experimental import pallas as pl
from jax.experimental.pallas import tpu as pltpu
from jax.sharding import PartitionSpec as P

LANES = 128
SUB = 8


def pack_column(values, lane):
    spot = lax.broadcasted_iota(jnp.int32, (SUB, LANES), 1)
    packed = jnp.zeros((SUB, LANES), jnp.float32)
    for group in range(values.shape[0] // SUB):
        tile = values[group * SUB:(group + 1) * SUB]
        turn = (group - lane) % LANES
        packed = jnp.where(spot == group, pltpu.roll(tile, turn, 1) if turn else tile, packed)
    return packed


def unpack_column(packed, first, count):
    tiles = []
    for group in range(first, first + count):
        turn = (-group) % LANES
        tiles.append(pltpu.roll(packed, turn, 1) if turn else packed)
    return jnp.concatenate(tiles, axis=0)


def kernel(
    sizes, moved_ref, east_ref, north_ref, lower_ref, pivot_ref, upper_ref, out_ref,
    north_buf, south_buf, wall_buf, west_out, east_out, west_buf, east_buf, inverse, advected,
    send_sem, recv_sem,
):
    count, levels, lat_count, lon_count = sizes
    rows = count * levels
    groups = rows // SUB
    lat, lon = lax.axis_index("lat"), lax.axis_index("lon")
    north, south = lax.rem(lat + 1, lat_count), lax.rem(lat + lat_count - 1, lat_count)
    east, west = lax.rem(lon + 1, lon_count), lax.rem(lon + lon_count - 1, lon_count)
    barrier = pltpu.get_barrier_semaphore()
    for device in ({"lat": north}, {"lat": south}, {"lon": east}, {"lon": west}):
        pl.semaphore_signal(barrier, inc=1, device_id=device, device_id_type=pl.DeviceIdType.MESH)

    own = [moved_ref[pl.ds(half, rows, stride=2), :] for half in range(2)]
    courant = [east_ref[pl.ds(half, levels, stride=2), :] for half in range(2)]
    west_out[...] = pack_column(jnp.concatenate([own[1], courant[1]], axis=0), LANES - 1)
    east_out[...] = pack_column(own[0], 0)
    pl.semaphore_wait(barrier, 4)

    def send(source, target, slot, device):
        copy = pltpu.make_async_remote_copy(
            src_ref=source, dst_ref=target, send_sem=send_sem.at[slot], recv_sem=recv_sem.at[slot],
            device_id=device, device_id_type=pl.DeviceIdType.MESH,
        )
        copy.start()
        return copy

    copies = [
        send(moved_ref, north_buf, 0, {"lat": south}),
        send(moved_ref, south_buf, 1, {"lat": north}),
        send(north_ref, wall_buf, 2, {"lat": north}),
        send(west_out, west_buf, 3, {"lon": east}),
        send(east_out, east_buf, 4, {"lon": west}),
    ]

    width = inverse.shape[1]
    place = lax.broadcasted_iota(jnp.int32, (1, width), 1)
    advected[rows:, :] = jnp.zeros((width - rows, 2 * LANES), jnp.float32)

    def product(block_ref, level, vectors):
        result = []
        for a in range(count):
            total = block_ref[a * count, level] * vectors[0]
            for b in range(1, count):
                total = total + block_ref[a * count + b, level] * vectors[b]
            result.append(total)
        return result

    def unit(level):
        return [jnp.where(place == b * levels + level, 1.0, 0.0).astype(jnp.float32) for b in range(count)]

    def keep(level, vectors):
        for a in range(count):
            inverse[pl.ds(a * levels + level, 1), :] = vectors[a]

    first = product(pivot_ref, 0, unit(0))
    keep(0, first)

    def forward_step(level, previous):
        coupled = product(lower_ref, level - 1, previous)
        right = [one - other for one, other in zip(unit(level), coupled)]
        current = product(pivot_ref, level, right)
        keep(level, current)
        return tuple(current)

    last = lax.fori_loop(1, levels, forward_step, tuple(first))

    def backward_step(step, following):
        level = levels - 2 - step
        coupled = product(upper_ref, level, following)
        current = [inverse[pl.ds(a * levels + level, 1), :] - coupled[a] for a in range(count)]
        keep(level, current)
        return tuple(current)

    lax.fori_loop(0, levels - 1, backward_step, last)

    for copy in copies:
        copy.wait()

    spot = lax.broadcasted_iota(jnp.int32, (rows, LANES), 1)
    shape = (count, levels, LANES)

    def upwind(speed, behind, ahead):
        return (
            jnp.maximum(speed, 0.0)[None] * behind.reshape(shape)
            + jnp.minimum(speed, 0.0)[None] * ahead.reshape(shape)
        ).reshape(rows, LANES)

    east_edge = unpack_column(east_buf[...], 0, groups)
    west_edge = unpack_column(west_buf[...], 0, groups)
    west_speed = unpack_column(west_buf[...], groups, levels // SUB)
    flux = [
        upwind(courant[0], own[0], pltpu.roll(jnp.where(spot == 0, own[1], own[0]), LANES - 1, 1)),
        upwind(courant[1], own[1], pltpu.roll(jnp.where(spot == 0, east_edge, own[1]), LANES - 1, 1)),
    ]
    from_west = [
        jnp.where(spot == 0, upwind(west_speed, west_edge, own[0]), pltpu.roll(flux[0], 1, 1)),
        pltpu.roll(jnp.where(spot == LANES - 1, flux[0], flux[1]), 1, 1),
    ]
    for half in range(2):
        part, level_part = pl.ds(half, rows, stride=2), pl.ds(half, levels, stride=2)
        north_wall = jnp.where(lat == lat_count - 1, 0.0, north_ref[level_part, :])
        south_wall = jnp.where(lat == 0, 0.0, wall_buf[level_part, :])
        to_north = upwind(north_wall, own[half], north_buf[part, :])
        from_south = upwind(south_wall, south_buf[part, :], own[half])
        advected[:rows, half * LANES:(half + 1) * LANES] = (
            own[half] - (flux[half] - from_west[half]) - (to_north - from_south)
        )
    solved = lax.dot_general(
        inverse[...], advected[...], (((1,), (0,)), ((), ())),
        precision=lax.Precision.HIGHEST, preferred_element_type=jnp.float32,
    )
    for half in range(2):
        out_ref[pl.ds(half, rows, stride=2), :] = solved[:, half * LANES:(half + 1) * LANES]


def body(fields, east_courant, north_courant, offsets, lower_blocks, pivot_inverse, upper_blocks):
    cycle_count = lax.axis_size("lon")
    band_count = lax.axis_size("lat")
    count, levels = fields.shape[:2]
    rows = count * levels
    displace = jnp.mod(offsets, cycle_count)

    def shift_by(step):
        pairs = [(place, (place + step) % cycle_count) for place in range(cycle_count)]

        def branch(block):
            return block if step == 0 else lax.ppermute(block, "lon", pairs)

        return branch

    moved = lax.switch(
        displace[0], [shift_by(step) for step in range(cycle_count)], fields.reshape(2 * rows, LANES)
    )
    width = -(-rows // 256) * 256
    vmem = pl.BlockSpec(memory_space=pltpu.VMEM)
    smem = pl.BlockSpec(memory_space=pltpu.SMEM)
    solved = pl.pallas_call(
        lambda *refs: kernel((count, levels, band_count, cycle_count), *refs),
        out_shape=jax.ShapeDtypeStruct((2 * rows, LANES), jnp.float32),
        in_specs=[vmem] * 3 + [smem] * 3,
        out_specs=vmem,
        scratch_shapes=[
            pltpu.VMEM((2 * rows, LANES), jnp.float32),
            pltpu.VMEM((2 * rows, LANES), jnp.float32),
            pltpu.VMEM((2 * levels, LANES), jnp.float32),
            pltpu.VMEM((SUB, LANES), jnp.float32),
            pltpu.VMEM((SUB, LANES), jnp.float32),
            pltpu.VMEM((SUB, LANES), jnp.float32),
            pltpu.VMEM((SUB, LANES), jnp.float32),
            pltpu.VMEM((rows, width), jnp.float32),
            pltpu.VMEM((width, 2 * LANES), jnp.float32),
            pltpu.SemaphoreType.DMA((5,)),
            pltpu.SemaphoreType.DMA((5,)),
        ],
        compiler_params=pltpu.CompilerParams(collective_id=0, has_side_effects=True),
    )(
        moved,
        east_courant.reshape(2 * levels, LANES),
        north_courant.reshape(2 * levels, LANES),
        lower_blocks.reshape(count * count, levels - 1),
        pivot_inverse.reshape(count * count, levels),
        upper_blocks.reshape(count * count, levels - 1),
    )
    return solved.reshape(fields.shape)


def solution(mesh):
    in_specs = (
        P(None, None, "lat", "lon"),
        P(None, "lat", "lon"),
        P(None, "lat", "lon"),
        P("lat"),
        P(None, None, None, "lat"),
        P(None, None, None, "lat"),
        P(None, None, None, "lat"),
    )
    out_specs = P(None, None, "lat", "lon")
    return jax.shard_map(body, mesh=mesh, in_specs=in_specs, out_specs=out_specs, check_vma=False)
```

time: 55.7 us -> 43.4 us (0.78)
  the two profiles are of different devices: /device:TPU:222 before, /device:TPU:6 now
where the time goes in v2:
time: 43.4 us; the launch traced here: 43 us
  Pallas kernels  24.3 us (56%)
  waiting for transfers between devices  7.95 us (18%)
  starting transfers between devices  5.89 us (14%)
  local copies, waits for them, and re-layouts  3.94 us (9%)
  between operations  0.76 us (2%)
    pallas_call x1, Pallas kernels, body(): pl.pallas_call(lambda *refs: kernel((count, levels, band_count, cycle_cou...  24.3 us
    ppermute x1, waiting for transfers between devices, branch(): return block if step == 0 else lax.ppermute(block, 'lon', pairs)  7.95 us
    ppermute x1, starting transfers between devices, branch(): return block if step == 0 else lax.ppermute(block, 'lon', pairs)  5.89 us
    unnamed x9, local copies, waits for them, and re-layouts  2.11 us
  transfers between devices with their start and end apart: 1, of which 1 were waited for; matrix products, arithmetic and copies ran while one was open for 0% of the time, Pallas kernels for 0%

profile of v2, /device:TPU:6, one launch (start us, length us, event | category | flops | bytes accessed | tf_op | source)
XLA Modules:
  0.0 43.0 jit_solution(8336230905390215889)
XLA Ops:
  0.0 0.0 copy-start
  0.7 0.2 copy-done
  0.9 0.0 copy-start.1
  0.9 13.9 %conditional.1 = (f32[320,128]{1,0:T(8,128)S(1)}) conditional(s32[]{:T(128)} %bitcast, f32[320,128]{1,0:T(8,128)S(1)} %bitcast.5, f32[320,128]{1,0:T(8,128)S(1)} %bitcast.6, f32[320,128]{1,0:T(8,128)S(1)} %bitcast.7, f32[320,128]{1,0:T(8,128)S(1)} %bitcast.8, f32[320,128]{1,0:T(8,128)S(1)} %bitcast.9, ...), branch_computations={%region_0.1_spmd, %region_1.2_spmd, %region_2.3_spmd, %region_3.4_... | conditional | bytes 983088 | solution.py:163
  0.9 5.9 %collective-permute-start.10 = (f32[320,128]{1,0:T(8,128)S(1)}, f32[320,128]{1,0:T(8,128)S(1)}, u32[]{:S(2)}, u32[]{:S(2)}) collective-permute-start(f32[320,128]{1,0:T(8,128)S(1)} %param.11), channel_id=1, source_target_pairs={{0,11},{1,12},{2,13},{3,14},{4,15},{5,0},{6,1},{7,2},{8,3},{9,4},{... | collective-permute-start | bytes 491528 | tf_op jit(solution)/shard_map/cond/branch_11_fun/ppermute | solution.py:159
  6.8 7.9 %collective-permute-done.10 = f32[320,128]{1,0:T(8,128)S(1)} collective-permute-done((f32[320,128]{1,0:T(8,128)S(1)}, f32[320,128]{1,0:T(8,128)S(1)}, u32[]{:S(2)}, u32[]{:S(2)}) %collective-permute-start.10) | collective-permute-done | bytes 163872 | tf_op jit(solution)/shard_map/cond/branch_11_fun/ppermute | solution.py:159
  14.8 0.0 copy-done.1
  14.9 0.0 copy-start.2
  14.9 0.6 %reshape.77.refs_3_ = f32[25,31]{1,0:T(8,128)} reshape(f32[5,5,31]{2,1,0:T(8,128)S(1)} %reduce) | data formatting | bytes 6200 | tf_op jit(solution)/shard_map/reshape | solution.py:192
  15.5 0.1 copy-done.2
  15.6 0.0 copy-start.3
  15.6 0.6 %reshape.78.refs_4_ = f32[25,32]{1,0:T(8,128)} reshape(f32[5,5,32]{2,1,0:T(8,128)S(1)} %reduce.1) | data formatting | bytes 6400 | tf_op jit(solution)/shard_map/reshape | solution.py:193
  16.2 0.1 copy-done.3
  16.4 0.6 %reshape.79.refs_5_ = f32[25,31]{1,0:T(8,128)} reshape(f32[5,5,31]{2,1,0:T(8,128)S(1)} %reduce.2) | data formatting | bytes 6200 | tf_op jit(solution)/shard_map/reshape | solution.py:194
  17.0 24.3 %shard_map.73 = f32[320,128]{1,0:T(8,128)} custom-call(f32[320,128]{1,0:T(8,128)S(1)} %get-tuple-element.38.refs_0_, f32[64,128]{1,0:T(8,128)} %bitcast.22, f32[64,128]{1,0:T(8,128)} %bitcast.23, f32[25,31]{1,0:T(8,128)} %reshape.77.refs_3_, f32[25,32]{1,0:T(8,128)} %reshape.78.refs_4_, f32[25,31]{1,0:T(8,128)} %reshape.79.refs_5_), custom_call_target="tpu_custom_call" | custom-call | tf_op jit(solution)/shard_map/pallas_call | solution.py:169
  41.3 1.7 %copy.32 = f32[5,32,1,256]{3,2,1,0:T(1,128)} copy(f32[5,32,1,256]{3,2,1,0:T(1,128)} %bitcast.21) | data formatting | bytes 327680
  (4 shorter events, 0.1 us)
Async XLA Ops:
  0.0 0.9 %copy-start = (f32[5,32,1,256]{3,2,1,0:T(1,128)S(1)}, f32[5,32,1,256]{3,2,1,0:T(1,128)}, u32[]{:S(2)}) copy-start(f32[5,32,1,256]{3,2,1,0:T(1,128)} %param.23) | copy-start | bytes 491524
  0.9 13.9 %copy-start.1 = (f32[5,5,31,1]{2,3,1,0:T(1,128)S(1)}, f32[5,5,31,1]{2,3,1,0:T(1,128)}, u32[]{:S(2)}) copy-start(f32[5,5,31,1]{2,3,1,0:T(1,128)} %param.27) | copy-start | bytes 9304
  0.9 13.9 %collective-permute-start.10 = (f32[320,128]{1,0:T(8,128)S(1)}, f32[320,128]{1,0:T(8,128)S(1)}, u32[]{:S(2)}, u32[]{:S(2)}) collective-permute-start(f32[320,128]{1,0:T(8,128)S(1)} %param.11), channel_id=1, source_target_pairs={{0,11},{1,12},{2,13},{3,14},{4,15},{5,0},{6,1},{7,2},{8,3},{9,4},{... | collective-permute-start | bytes 491528 | tf_op jit(solution)/shard_map/cond/branch_11_fun/ppermute | solution.py:159
  14.9 0.7 %copy-start.2 = (f32[5,5,32,1]{2,3,1,0:T(1,128)S(1)}, f32[5,5,32,1]{2,3,1,0:T(1,128)}, u32[]{:S(2)}) copy-start(f32[5,5,32,1]{2,3,1,0:T(1,128)} %param.28) | copy-start | bytes 9604
  15.6 0.7 %copy-start.3 = (f32[5,5,31,1]{2,3,1,0:T(1,128)S(1)}, f32[5,5,31,1]{2,3,1,0:T(1,128)}, u32[]{:S(2)}) copy-start(f32[5,5,31,1]{2,3,1,0:T(1,128)} %param.29) | copy-start | bytes 9304

commit v3 on v2

--- a/solution.py
+++ b/solution.py
@@ -28,8 +28,8 @@
 
 
 def kernel(
-    sizes, moved_ref, east_ref, north_ref, lower_ref, pivot_ref, upper_ref, out_ref,
-    north_buf, south_buf, wall_buf, west_out, east_out, west_buf, east_buf, inverse, advected,
+    sizes, moved_ref, east_ref, north_ref, lower_ref, pivot_ref, upper_ref, inverse, advected,
+    north_buf, south_buf, wall_buf, west_out, east_out, west_buf, east_buf, base,
     send_sem, recv_sem,
 ):
     count, levels, lat_count, lon_count = sizes
@@ -71,9 +71,9 @@
     def product(block_ref, level, vectors):
         result = []
         for a in range(count):
-            total = block_ref[a * count, level] * vectors[0]
+            total = block_ref[a * count, 0, level] * vectors[0]
             for b in range(1, count):
-                total = total + block_ref[a * count + b, level] * vectors[b]
+                total = total + block_ref[a * count + b, 0, level] * vectors[b]
             result.append(total)
         return result
 
@@ -105,7 +105,7 @@
 
     lax.fori_loop(0, levels - 1, backward_step, last)
 
-    for copy in copies:
+    for copy in copies[2:]:
         copy.wait()
 
     spot = lax.broadcasted_iota(jnp.int32, (rows, LANES), 1)
@@ -129,20 +129,26 @@
         pltpu.roll(jnp.where(spot == LANES - 1, flux[0], flux[1]), 1, 1),
     ]
     for half in range(2):
+        base[half] = own[half] - (flux[half] - from_west[half])
+    for copy in copies[:2]:
+        copy.wait()
+    for half in range(2):
         part, level_part = pl.ds(half, rows, stride=2), pl.ds(half, levels, stride=2)
         north_wall = jnp.where(lat == lat_count - 1, 0.0, north_ref[level_part, :])
         south_wall = jnp.where(lat == 0, 0.0, wall_buf[level_part, :])
-        to_north = upwind(north_wall, own[half], north_buf[part, :])
-        from_south = upwind(south_wall, south_buf[part, :], own[half])
-        advected[:rows, half * LANES:(half + 1) * LANES] = (
-            own[half] - (flux[half] - from_west[half]) - (to_north - from_south)
-        )
+        middle = moved_ref[part, :]
+        to_north = upwind(north_wall, middle, north_buf[part, :])
+        from_south = upwind(south_wall, south_buf[part, :], middle)
+        advected[:rows, half * LANES:(half + 1) * LANES] = base[half] - (to_north - from_south)
+
+
+def apply_inverse(inverse, advected, out_ref):
     solved = lax.dot_general(
         inverse[...], advected[...], (((1,), (0,)), ((), ())),
         precision=lax.Precision.HIGHEST, preferred_element_type=jnp.float32,
     )
     for half in range(2):
-        out_ref[pl.ds(half, rows, stride=2), :] = solved[:, half * LANES:(half + 1) * LANES]
+        out_ref[pl.ds(half, inverse.shape[0], stride=2), :] = solved[:, half * LANES:(half + 1) * LANES]
 
 
 def body(fields, east_courant, north_courant, offsets, lower_blocks, pivot_inverse, upper_blocks):
@@ -166,11 +172,14 @@
     width = -(-rows // 256) * 256
     vmem = pl.BlockSpec(memory_space=pltpu.VMEM)
     smem = pl.BlockSpec(memory_space=pltpu.SMEM)
-    solved = pl.pallas_call(
+    inverse, advected = pl.pallas_call(
         lambda *refs: kernel((count, levels, band_count, cycle_count), *refs),
-        out_shape=jax.ShapeDtypeStruct((2 * rows, LANES), jnp.float32),
+        out_shape=(
+            jax.ShapeDtypeStruct((rows, width), jnp.float32),
+            jax.ShapeDtypeStruct((width, 2 * LANES), jnp.float32),
+        ),
         in_specs=[vmem] * 3 + [smem] * 3,
-        out_specs=vmem,
+        out_specs=(vmem, vmem),
         scratch_shapes=[
             pltpu.VMEM((2 * rows, LANES), jnp.float32),
             pltpu.VMEM((2 * rows, LANES), jnp.float32),
@@ -179,20 +188,28 @@
             pltpu.VMEM((SUB, LANES), jnp.float32),
             pltpu.VMEM((SUB, LANES), jnp.float32),
             pltpu.VMEM((SUB, LANES), jnp.float32),
-            pltpu.VMEM((rows, width), jnp.float32),
-            pltpu.VMEM((width, 2 * LANES), jnp.float32),
+            pltpu.VMEM((2, rows, LANES), jnp.float32),
             pltpu.SemaphoreType.DMA((5,)),
             pltpu.SemaphoreType.DMA((5,)),
         ],
-        compiler_params=pltpu.CompilerParams(collective_id=0, has_side_effects=True),
+        compiler_params=pltpu.CompilerParams(
+            collective_id=0, has_side_effects=True, vmem_limit_bytes=8 * 1024 * 1024
+        ),
     )(
         moved,
         east_courant.reshape(2 * levels, LANES),
         north_courant.reshape(2 * levels, LANES),
-        lower_blocks.reshape(count * count, levels - 1),
-        pivot_inverse.reshape(count * count, levels),
-        upper_blocks.reshape(count * count, levels - 1),
-    )
+        jnp.swapaxes(lower_blocks, 2, 3).reshape(count * count, 1, levels - 1),
+        jnp.swapaxes(pivot_inverse, 2, 3).reshape(count * count, 1, levels),
+        jnp.swapaxes(upper_blocks, 2, 3).reshape(count * count, 1, levels - 1),
+    )
+    solved = pl.pallas_call(
+        apply_inverse,
+        out_shape=jax.ShapeDtypeStruct((2 * rows, LANES), jnp.float32),
+        in_specs=[vmem] * 2,
+        out_specs=vmem,
+        compiler_params=pltpu.CompilerParams(vmem_limit_bytes=8 * 1024 * 1024),
+    )(inverse, advected)
     return solved.reshape(fields.shape)
 
 

time: 43.4 us -> 39.9 us (0.919)
  the two profiles are of different devices: /device:TPU:6 before, /device:TPU:2 now
where the time goes in v3:
time: 39.9 us; the launch traced here: 39.6 us
  Pallas kernels  27.7 us (69%)
  waiting for transfers between devices  7.27 us (18%)
  starting transfers between devices  3.59 us (9%)
  between operations  0.78 us (2%)
    pallas_call x1, Pallas kernels, body(): pl.pallas_call(lambda *refs: kernel((count, levels, band_count, cycle_cou...  26.7 us
    ppermute x1, waiting for transfers between devices, branch(): return block if step == 0 else lax.ppermute(block, 'lon', pairs)  7.27 us
    ppermute x1, starting transfers between devices, branch(): return block if step == 0 else lax.ppermute(block, 'lon', pairs)  3.59 us
    pallas_call x1, Pallas kernels, body(): pl.pallas_call(apply_inverse, out_shape=jax.ShapeDtypeStruct((2 * rows, L...  0.98 us
  transfers between devices with their start and end apart: 1, of which 1 were waited for; matrix products, arithmetic and copies ran while one was open for 0% of the time, Pallas kernels for 0%

profile of v3, /device:TPU:2, one launch (start us, length us, event | category | flops | bytes accessed | tf_op | source)
XLA Modules:
  0.0 39.6 jit_solution(13790043763508819825)
XLA Ops:
  0.0 0.0 copy-start.5
  0.7 0.2 copy-done.5
  0.9 0.0 copy-start
  0.9 0.0 copy-start.1
  0.9 0.0 copy-start.2
  0.9 0.0 copy-start.3
  0.9 0.0 copy-start.4
  1.0 10.9 %conditional.1 = (f32[320,128]{1,0:T(8,128)S(1)}) conditional(s32[]{:T(128)} %bitcast, f32[320,128]{1,0:T(8,128)S(1)} %bitcast.13, f32[320,128]{1,0:T(8,128)S(1)} %bitcast.14, f32[320,128]{1,0:T(8,128)S(1)} %bitcast.15, f32[320,128]{1,0:T(8,128)S(1)} %bitcast.16, f32[320,128]{1,0:T(8,128)S(1)} %bitcast.17, ...), branch_computations={%region_0.1_spmd, %region_1.2_spmd, %region_2.3_spmd, %region_3.4_... | conditional | bytes 983088 | solution.py:169
  1.0 3.6 %collective-permute-start.2 = (f32[320,128]{1,0:T(8,128)S(1)}, f32[320,128]{1,0:T(8,128)S(1)}, u32[]{:S(2)}, u32[]{:S(2)}) collective-permute-start(f32[320,128]{1,0:T(8,128)S(1)} %param.3), channel_id=1, source_target_pairs={{0,3},{1,4},{2,5},{3,6},{4,7},{5,8},{6,9},{7,10},{8,11},{9,12},{10... | collective-permute-start | bytes 491528 | tf_op jit(solution)/shard_map/cond/branch_3_fun/ppermute | solution.py:165
  4.6 7.3 %collective-permute-done.2 = f32[320,128]{1,0:T(8,128)S(1)} collective-permute-done((f32[320,128]{1,0:T(8,128)S(1)}, f32[320,128]{1,0:T(8,128)S(1)}, u32[]{:S(2)}, u32[]{:S(2)}) %collective-permute-start.2) | collective-permute-done | bytes 163872 | tf_op jit(solution)/shard_map/cond/branch_3_fun/ppermute | solution.py:165
  11.9 0.0 copy-done
  11.9 0.0 copy-done.1
  11.9 0.0 copy-done.2
  11.9 0.0 copy-done.3
  11.9 0.0 copy-done.4
  11.9 26.7 %shard_map.73 = (f32[160,256]{1,0:T(8,128)S(1)}, f32[256,256]{1,0:T(8,128)S(1)}) custom-call(f32[320,128]{1,0:T(8,128)S(1)} %get-tuple-element.42.refs_0_, f32[64,128]{1,0:T(8,128)S(1)} %bitcast.8, f32[64,128]{1,0:T(8,128)S(1)} %bitcast.9, f32[25,1,31]{2,1,0:T(1,128)S(1)} %bitcast.10, f32[25,1,32]{2,1,0:T(1,128)S(1)} %bitcast.11, f32[25,1,31]{2,1,0:T(1,128)S(1)} %bitcast.12), custom_call_target="tpu_custom_call" | custom-call | tf_op jit(solution)/shard_map/pallas_call | solution.py:175
  38.7 1.0 %shard_map.74 = f32[320,128]{1,0:T(8,128)} custom-call(f32[160,256]{1,0:T(8,128)S(1)} %get-tuple-element.40.inverse, f32[256,256]{1,0:T(8,128)S(1)} %get-tuple-element.41.advected), custom_call_target="tpu_custom_call" | custom-call | tf_op jit(solution)/shard_map/pallas_call | solution.py:206
  (1 shorter events, 0.0 us)
Async XLA Ops:
  0.0 0.9 %copy-start.5 = (f32[5,32,1,256]{3,2,1,0:T(1,128)S(1)}, f32[5,32,1,256]{3,2,1,0:T(1,128)}, u32[]{:S(2)}) copy-start(f32[5,32,1,256]{3,2,1,0:T(1,128)} %param.23) | copy-start | bytes 491524
  0.9 11.0 %copy-start = (f32[32,1,256]{2,1,0:T(1,128)S(1)}, f32[32,1,256]{2,1,0:T(1,128)}, u32[]{:S(2)}) copy-start(f32[32,1,256]{2,1,0:T(1,128)} %param.24) | copy-start | bytes 98308
  0.9 11.0 %copy-start.1 = (f32[32,1,256]{2,1,0:T(1,128)S(1)}, f32[32,1,256]{2,1,0:T(1,128)}, u32[]{:S(2)}) copy-start(f32[32,1,256]{2,1,0:T(1,128)} %param.25) | copy-start | bytes 98308
  0.9 11.0 %copy-start.2 = (f32[5,5,31,1]{2,3,1,0:T(1,128)S(1)}, f32[5,5,31,1]{2,3,1,0:T(1,128)}, u32[]{:S(2)}) copy-start(f32[5,5,31,1]{2,3,1,0:T(1,128)} %param.27) | copy-start | bytes 9304
  0.9 11.0 %copy-start.3 = (f32[5,5,32,1]{2,3,1,0:T(1,128)S(1)}, f32[5,5,32,1]{2,3,1,0:T(1,128)}, u32[]{:S(2)}) copy-start(f32[5,5,32,1]{2,3,1,0:T(1,128)} %param.28) | copy-start | bytes 9604
  0.9 11.0 %copy-start.4 = (f32[5,5,31,1]{2,3,1,0:T(1,128)S(1)}, f32[5,5,31,1]{2,3,1,0:T(1,128)}, u32[]{:S(2)}) copy-start(f32[5,5,31,1]{2,3,1,0:T(1,128)} %param.29) | copy-start | bytes 9304
  1.0 10.9 %collective-permute-start.2 = (f32[320,128]{1,0:T(8,128)S(1)}, f32[320,128]{1,0:T(8,128)S(1)}, u32[]{:S(2)}, u32[]{:S(2)}) collective-permute-start(f32[320,128]{1,0:T(8,128)S(1)} %param.3), channel_id=1, source_target_pairs={{0,3},{1,4},{2,5},{3,6},{4,7},{5,8},{6,9},{7,10},{8,11},{9,12},{10... | collective-permute-start | bytes 491528 | tf_op jit(solution)/shard_map/cond/branch_3_fun/ppermute | solution.py:165

commit v4 on v3

--- a/solution.py
+++ b/solution.py
@@ -29,7 +29,7 @@
 
 def kernel(
     sizes, moved_ref, east_ref, north_ref, lower_ref, pivot_ref, upper_ref, inverse, advected,
-    north_buf, south_buf, wall_buf, west_out, east_out, west_buf, east_buf, base,
+    lat_buf, wall_buf, west_out, east_out, west_buf, east_buf, base,
     send_sem, recv_sem,
 ):
     count, levels, lat_count, lon_count = sizes
@@ -56,12 +56,14 @@
         copy.start()
         return copy
 
+    far = lax.rem(lat, 2)
+    near = 1 - far
     copies = [
-        send(moved_ref, north_buf, 0, {"lat": south}),
-        send(moved_ref, south_buf, 1, {"lat": north}),
-        send(north_ref, wall_buf, 2, {"lat": north}),
         send(west_out, west_buf, 3, {"lon": east}),
         send(east_out, east_buf, 4, {"lon": west}),
+        send(moved_ref, lat_buf.at[far], far, {"lat": jnp.where(far == 1, north, south)}),
+        send(north_ref, wall_buf, 2, {"lat": north}),
+        send(moved_ref, lat_buf.at[near], near, {"lat": jnp.where(far == 1, south, north)}),
     ]
 
     width = inverse.shape[1]
@@ -105,7 +107,7 @@
 
     lax.fori_loop(0, levels - 1, backward_step, last)
 
-    for copy in copies[2:]:
+    for copy in copies[:2]:
         copy.wait()
 
     spot = lax.broadcasted_iota(jnp.int32, (rows, LANES), 1)
@@ -130,15 +132,15 @@
     ]
     for half in range(2):
         base[half] = own[half] - (flux[half] - from_west[half])
-    for copy in copies[:2]:
+    for copy in copies[2:]:
         copy.wait()
     for half in range(2):
         part, level_part = pl.ds(half, rows, stride=2), pl.ds(half, levels, stride=2)
         north_wall = jnp.where(lat == lat_count - 1, 0.0, north_ref[level_part, :])
         south_wall = jnp.where(lat == 0, 0.0, wall_buf[level_part, :])
         middle = moved_ref[part, :]
-        to_north = upwind(north_wall, middle, north_buf[part, :])
-        from_south = upwind(south_wall, south_buf[part, :], middle)
+        to_north = upwind(north_wall, middle, lat_buf[0, part, :])
+        from_south = upwind(south_wall, lat_buf[1, part, :], middle)
         advected[:rows, half * LANES:(half + 1) * LANES] = base[half] - (to_north - from_south)
 
 
@@ -181,8 +183,7 @@
         in_specs=[vmem] * 3 + [smem] * 3,
         out_specs=(vmem, vmem),
         scratch_shapes=[
-            pltpu.VMEM((2 * rows, LANES), jnp.float32),
-            pltpu.VMEM((2 * rows, LANES), jnp.float32),
+            pltpu.VMEM((2, 2 * rows, LANES), jnp.float32),
             pltpu.VMEM((2 * levels, LANES), jnp.float32),
             pltpu.VMEM((SUB, LANES), jnp.float32),
             pltpu.VMEM((SUB, LANES), jnp.float32),

time: 39.9 us -> 40.9 us (1.025)
  Pallas kernels: 27.7 us -> 39 us
  waiting for transfers between devices: 7.27 us -> 0 us
  starting transfers between devices: 3.59 us -> 0 us
  local copies, waits for them, and re-layouts: 0.26 us -> 0.94 us
    pallas_call x1, Pallas kernels: 26.7 us -> 38 us  [body(): pl.pallas_call(lambda *refs: kernel((count, levels, band_count, cycle_cou...]
    ppermute x1 -> x0, waiting for transfers between devices: 7.27 us -> none  [branch(): return block if step == 0 else lax.ppermute(block, 'lon', pairs)]
    ppermute x1 -> x0, starting transfers between devices: 3.59 us -> none  [branch(): return block if step == 0 else lax.ppermute(block, 'lon', pairs)]
    unnamed x12, local copies, waits for them, and re-layouts: 0.24 us -> 0.94 us
  transfers between devices with their start and end apart: 1 -> 0, of which waited for: 1 -> 0; matrix products, arithmetic and copies ran while one was open for 0% -> 0% of each run, Pallas kernels for 0% -> 0%
where the time goes in v4:
time: 40.9 us; the launch traced here: 40.7 us
  Pallas kernels  39 us (95%)
  local copies, waits for them, and re-layouts  0.94 us (2%)
  between operations  0.74 us (2%)
    pallas_call x1, Pallas kernels, body(): pl.pallas_call(lambda *refs: kernel((count, levels, band_count, cycle_cou...  38 us
    pallas_call x1, Pallas kernels, body(): pl.pallas_call(apply_inverse, out_shape=jax.ShapeDtypeStruct((2 * rows, L...  0.97 us
    unnamed x12, local copies, waits for them, and re-layouts  0.94 us

profile of v4, /device:TPU:2, one launch (start us, length us, event | category | flops | bytes accessed | tf_op | source)
XLA Modules:
  0.0 40.7 jit_solution(1112548085113692086)
XLA Ops:
  0.0 0.0 copy-start.5
  0.7 0.2 copy-done.5
  0.9 0.0 copy-start
  0.9 0.0 copy-start.1
  0.9 0.0 copy-start.2
  0.9 0.0 copy-start.3
  0.9 0.0 copy-start.4
  1.0 0.7 %copy-done = f32[32,1,256]{2,1,0:T(1,128)S(1)} copy-done((f32[32,1,256]{2,1,0:T(1,128)S(1)}, f32[32,1,256]{2,1,0:T(1,128)}, u32[]{:S(2)}) %copy-start) | copy-done | bytes 32792
  1.7 0.0 copy-done.1
  1.7 0.0 copy-done.2
  1.7 0.0 copy-done.3
  1.7 0.0 copy-done.4
  1.7 38.0 %shard_map.73 = (f32[160,256]{1,0:T(8,128)S(1)}, f32[256,256]{1,0:T(8,128)S(1)}) custom-call(f32[320,128]{1,0:T(8,128)S(1)} %get-tuple-element.42.refs_0_, f32[64,128]{1,0:T(8,128)S(1)} %bitcast.8, f32[64,128]{1,0:T(8,128)S(1)} %bitcast.9, f32[25,1,31]{2,1,0:T(1,128)S(1)} %bitcast.10, f32[25,1,32]{2,1,0:T(1,128)S(1)} %bitcast.11, f32[25,1,31]{2,1,0:T(1,128)S(1)} %bitcast.12), custom_call_target="tpu_custom_call" | custom-call | tf_op jit(solution)/shard_map/pallas_call | solution.py:177
  39.7 1.0 %shard_map.74 = f32[320,128]{1,0:T(8,128)} custom-call(f32[160,256]{1,0:T(8,128)S(1)} %get-tuple-element.40.inverse, f32[256,256]{1,0:T(8,128)S(1)} %get-tuple-element.41.advected), custom_call_target="tpu_custom_call" | custom-call | tf_op jit(solution)/shard_map/pallas_call | solution.py:207
  (1 shorter events, 0.0 us)
Async XLA Ops:
  0.0 0.9 %copy-start.5 = (f32[5,32,1,256]{3,2,1,0:T(1,128)S(1)}, f32[5,32,1,256]{3,2,1,0:T(1,128)}, u32[]{:S(2)}) copy-start(f32[5,32,1,256]{3,2,1,0:T(1,128)} %param.23) | copy-start | bytes 491524
  0.9 0.8 %copy-start = (f32[32,1,256]{2,1,0:T(1,128)S(1)}, f32[32,1,256]{2,1,0:T(1,128)}, u32[]{:S(2)}) copy-start(f32[32,1,256]{2,1,0:T(1,128)} %param.24) | copy-start | bytes 98308
  0.9 0.8 %copy-start.1 = (f32[32,1,256]{2,1,0:T(1,128)S(1)}, f32[32,1,256]{2,1,0:T(1,128)}, u32[]{:S(2)}) copy-start(f32[32,1,256]{2,1,0:T(1,128)} %param.25) | copy-start | bytes 98308
  0.9 0.8 %copy-start.2 = (f32[5,5,31,1]{2,3,1,0:T(1,128)S(1)}, f32[5,5,31,1]{2,3,1,0:T(1,128)}, u32[]{:S(2)}) copy-start(f32[5,5,31,1]{2,3,1,0:T(1,128)} %param.27) | copy-start | bytes 9304
  0.9 0.8 %copy-start.3 = (f32[5,5,32,1]{2,3,1,0:T(1,128)S(1)}, f32[5,5,32,1]{2,3,1,0:T(1,128)}, u32[]{:S(2)}) copy-start(f32[5,5,32,1]{2,3,1,0:T(1,128)} %param.28) | copy-start | bytes 9604
  0.9 0.8 %copy-start.4 = (f32[5,5,31,1]{2,3,1,0:T(1,128)S(1)}, f32[5,5,31,1]{2,3,1,0:T(1,128)}, u32[]{:S(2)}) copy-start(f32[5,5,31,1]{2,3,1,0:T(1,128)} %param.29) | copy-start | bytes 9304

commit v5 on v3

--- a/solution.py
+++ b/solution.py
@@ -39,30 +39,68 @@
     north, south = lax.rem(lat + 1, lat_count), lax.rem(lat + lat_count - 1, lat_count)
     east, west = lax.rem(lon + 1, lon_count), lax.rem(lon + lon_count - 1, lon_count)
     barrier = pltpu.get_barrier_semaphore()
-    for device in ({"lat": north}, {"lat": south}, {"lon": east}, {"lon": west}):
+    inside_north, inside_south = lat < lat_count - 1, lat > 0
+
+    def greet(device):
         pl.semaphore_signal(barrier, inc=1, device_id=device, device_id_type=pl.DeviceIdType.MESH)
+
+    greet({"lon": east})
+    greet({"lon": west})
+
+    @pl.when(inside_north)
+    def _():
+        greet({"lat": north})
+
+    @pl.when(inside_south)
+    def _():
+        greet({"lat": south})
+
 
     own = [moved_ref[pl.ds(half, rows, stride=2), :] for half in range(2)]
     courant = [east_ref[pl.ds(half, levels, stride=2), :] for half in range(2)]
     west_out[...] = pack_column(jnp.concatenate([own[1], courant[1]], axis=0), LANES - 1)
     east_out[...] = pack_column(own[0], 0)
-    pl.semaphore_wait(barrier, 4)
-
-    def send(source, target, slot, device):
-        copy = pltpu.make_async_remote_copy(
+    interior = jnp.logical_and(inside_north, inside_south)
+
+    @pl.when(interior)
+    def _():
+        pl.semaphore_wait(barrier, 4)
+
+    @pl.when(jnp.logical_not(interior))
+    def _():
+        pl.semaphore_wait(barrier, 3)
+
+
+    def link(source, target, slot, device):
+        return pltpu.make_async_remote_copy(
             src_ref=source, dst_ref=target, send_sem=send_sem.at[slot], recv_sem=recv_sem.at[slot],
             device_id=device, device_id_type=pl.DeviceIdType.MESH,
         )
+
+    to_south = link(moved_ref, north_buf, 0, {"lat": south})
+    to_north_row = link(moved_ref, south_buf, 1, {"lat": north})
+    wall = link(north_ref, wall_buf, 2, {"lat": north})
+    edges = [link(west_out, west_buf, 3, {"lon": east}), link(east_out, east_buf, 4, {"lon": west})]
+    for copy in edges:
         copy.start()
-        return copy
-
-    copies = [
-        send(moved_ref, north_buf, 0, {"lat": south}),
-        send(moved_ref, south_buf, 1, {"lat": north}),
-        send(north_ref, wall_buf, 2, {"lat": north}),
-        send(west_out, west_buf, 3, {"lon": east}),
-        send(east_out, east_buf, 4, {"lon": west}),
-    ]
+
+    @pl.when(inside_south)
+    def _():
+        to_south.start()
+
+    @pl.when(inside_north)
+    def _():
+        to_north_row.start()
+        wall.start()
+
+    @pl.when(jnp.logical_not(inside_north))
+    def _():
+        north_buf[...] = jnp.zeros_like(north_buf)
+
+    @pl.when(jnp.logical_not(inside_south))
+    def _():
+        south_buf[...] = jnp.zeros_like(south_buf)
+        wall_buf[...] = jnp.zeros_like(wall_buf)
 
     width = inverse.shape[1]
     place = lax.broadcasted_iota(jnp.int32, (1, width), 1)
@@ -105,7 +143,7 @@
 
     lax.fori_loop(0, levels - 1, backward_step, last)
 
-    for copy in copies[2:]:
+    for copy in edges:
         copy.wait()
 
     spot = lax.broadcasted_iota(jnp.int32, (rows, LANES), 1)
@@ -130,8 +168,19 @@
     ]
     for half in range(2):
         base[half] = own[half] - (flux[half] - from_west[half])
-    for copy in copies[:2]:
-        copy.wait()
+
+    @pl.when(inside_south)
+    def _():
+        to_south.wait_send()
+        to_north_row.wait_recv()
+        wall.wait_recv()
+
+    @pl.when(inside_north)
+    def _():
+        to_north_row.wait_send()
+        wall.wait_send()
+        to_south.wait_recv()
+
     for half in range(2):
         part, level_part = pl.ds(half, rows, stride=2), pl.ds(half, levels, stride=2)
         north_wall = jnp.where(lat == lat_count - 1, 0.0, north_ref[level_part, :])

time: 39.9 us -> 32.7 us (0.82)
  the two profiles are of different devices: /device:TPU:2 before, /device:TPU:65 now
where the time goes in v5:
time: 32.7 us; the launch traced here: 32.5 us
  Pallas kernels  20.5 us (63%)
  waiting for transfers between devices  6.54 us (20%)
  starting transfers between devices  4.35 us (13%)
  between operations  0.78 us (2%)
    pallas_call x1, Pallas kernels, body(): pl.pallas_call(lambda *refs: kernel((count, levels, band_count, cycle_cou...  19.6 us
    ppermute x1, waiting for transfers between devices, branch(): return block if step == 0 else lax.ppermute(block, 'lon', pairs)  6.54 us
    ppermute x1, starting transfers between devices, branch(): return block if step == 0 else lax.ppermute(block, 'lon', pairs)  4.35 us
    pallas_call x1, Pallas kernels, body(): pl.pallas_call(apply_inverse, out_shape=jax.ShapeDtypeStruct((2 * rows, L...  0.97 us
  transfers between devices with their start and end apart: 1, of which 1 were waited for; matrix products, arithmetic and copies ran while one was open for 0% of the time, Pallas kernels for 0%

profile of v5, /device:TPU:65, one launch (start us, length us, event | category | flops | bytes accessed | tf_op | source)
XLA Modules:
  0.0 32.5 jit_solution(13263879158907370677)
XLA Ops:
  0.0 0.0 copy-start.5
  0.7 0.2 copy-done.5
  0.9 0.0 copy-start
  0.9 0.0 copy-start.1
  0.9 0.0 copy-start.2
  0.9 0.0 copy-start.3
  0.9 0.0 copy-start.4
  1.0 11.0 %conditional.1 = (f32[320,128]{1,0:T(8,128)S(1)}) conditional(s32[]{:T(128)} %bitcast, f32[320,128]{1,0:T(8,128)S(1)} %bitcast.13, f32[320,128]{1,0:T(8,128)S(1)} %bitcast.14, f32[320,128]{1,0:T(8,128)S(1)} %bitcast.15, f32[320,128]{1,0:T(8,128)S(1)} %bitcast.16, f32[320,128]{1,0:T(8,128)S(1)} %bitcast.17, ...), branch_computations={%region_0.1_spmd, %region_1.2_spmd, %region_2.3_spmd, %region_3.4_... | conditional | bytes 983088 | solution.py:218
  1.0 4.3 %collective-permute-start.7 = (f32[320,128]{1,0:T(8,128)S(1)}, f32[320,128]{1,0:T(8,128)S(1)}, u32[]{:S(2)}, u32[]{:S(2)}) collective-permute-start(f32[320,128]{1,0:T(8,128)S(1)} %param.8), channel_id=1, source_target_pairs={{0,8},{1,9},{2,10},{3,11},{4,12},{5,13},{6,14},{7,15},{8,0},{9,1},... | collective-permute-start | bytes 491528 | tf_op jit(solution)/shard_map/cond/branch_8_fun/ppermute | solution.py:214
  5.3 6.5 %collective-permute-done.7 = f32[320,128]{1,0:T(8,128)S(1)} collective-permute-done((f32[320,128]{1,0:T(8,128)S(1)}, f32[320,128]{1,0:T(8,128)S(1)}, u32[]{:S(2)}, u32[]{:S(2)}) %collective-permute-start.7) | collective-permute-done | bytes 163872 | tf_op jit(solution)/shard_map/cond/branch_8_fun/ppermute | solution.py:214
  11.9 0.0 copy-done
  11.9 0.0 copy-done.1
  11.9 0.0 copy-done.2
  12.0 0.0 copy-done.3
  12.0 0.0 copy-done.4
  12.0 19.6 %shard_map.73 = (f32[160,256]{1,0:T(8,128)S(1)}, f32[256,256]{1,0:T(8,128)S(1)}) custom-call(f32[320,128]{1,0:T(8,128)S(1)} %get-tuple-element.42.refs_0_, f32[64,128]{1,0:T(8,128)S(1)} %bitcast.8, f32[64,128]{1,0:T(8,128)S(1)} %bitcast.9, f32[25,1,31]{2,1,0:T(1,128)S(1)} %bitcast.10, f32[25,1,32]{2,1,0:T(1,128)S(1)} %bitcast.11, f32[25,1,31]{2,1,0:T(1,128)S(1)} %bitcast.12), custom_call_target="tpu_custom_call" | custom-call | tf_op jit(solution)/shard_map/pallas_call | solution.py:224
  31.5 1.0 %shard_map.74 = f32[320,128]{1,0:T(8,128)} custom-call(f32[160,256]{1,0:T(8,128)S(1)} %get-tuple-element.40.inverse, f32[256,256]{1,0:T(8,128)S(1)} %get-tuple-element.41.advected), custom_call_target="tpu_custom_call" | custom-call | tf_op jit(solution)/shard_map/pallas_call | solution.py:255
  (1 shorter events, 0.0 us)
Async XLA Ops:
  0.0 0.9 %copy-start.5 = (f32[5,32,1,256]{3,2,1,0:T(1,128)S(1)}, f32[5,32,1,256]{3,2,1,0:T(1,128)}, u32[]{:S(2)}) copy-start(f32[5,32,1,256]{3,2,1,0:T(1,128)} %param.23) | copy-start | bytes 491524
  0.9 11.0 %copy-start = (f32[32,1,256]{2,1,0:T(1,128)S(1)}, f32[32,1,256]{2,1,0:T(1,128)}, u32[]{:S(2)}) copy-start(f32[32,1,256]{2,1,0:T(1,128)} %param.24) | copy-start | bytes 98308
  0.9 11.0 %copy-start.1 = (f32[32,1,256]{2,1,0:T(1,128)S(1)}, f32[32,1,256]{2,1,0:T(1,128)}, u32[]{:S(2)}) copy-start(f32[32,1,256]{2,1,0:T(1,128)} %param.25) | copy-start | bytes 98308
  0.9 11.0 %copy-start.2 = (f32[5,5,31,1]{2,3,1,0:T(1,128)S(1)}, f32[5,5,31,1]{2,3,1,0:T(1,128)}, u32[]{:S(2)}) copy-start(f32[5,5,31,1]{2,3,1,0:T(1,128)} %param.27) | copy-start | bytes 9304
  0.9 11.0 %copy-start.3 = (f32[5,5,32,1]{2,3,1,0:T(1,128)S(1)}, f32[5,5,32,1]{2,3,1,0:T(1,128)}, u32[]{:S(2)}) copy-start(f32[5,5,32,1]{2,3,1,0:T(1,128)} %param.28) | copy-start | bytes 9604
  0.9 11.0 %copy-start.4 = (f32[5,5,31,1]{2,3,1,0:T(1,128)S(1)}, f32[5,5,31,1]{2,3,1,0:T(1,128)}, u32[]{:S(2)}) copy-start(f32[5,5,31,1]{2,3,1,0:T(1,128)} %param.29) | copy-start | bytes 9304
  1.0 10.9 %collective-permute-start.7 = (f32[320,128]{1,0:T(8,128)S(1)}, f32[320,128]{1,0:T(8,128)S(1)}, u32[]{:S(2)}, u32[]{:S(2)}) collective-permute-start(f32[320,128]{1,0:T(8,128)S(1)} %param.8), channel_id=1, source_target_pairs={{0,8},{1,9},{2,10},{3,11},{4,12},{5,13},{6,14},{7,15},{8,0},{9,1},... | collective-permute-start | bytes 491528 | tf_op jit(solution)/shard_map/cond/branch_8_fun/ppermute | solution.py:214
